TPU v7x, 32 devices: a whole 2x2x4 slice. The times are simulated.
32 devices in a mesh: wide: 16 (over z, y, core), blk: 2 (over x).
Axes of the slice: x: 2, y: 2, z: 4, core: 2. Of those that a mesh axis runs over, the one named last changes fastest.
Arguments:
- position: float32 [3, 4096], P(None, ('wide', 'blk')), may hold values from -1 to 1, as said below
- order_field: float32 [12, 4096], P(None, ('wide', 'blk')), may hold values from -1.5 to 1.5
- cell_area: float32 [4096], P(('wide', 'blk')), may hold values from 0.5 to 2
- slot_vertex: int32 [16, 2, 16, 24], P('wide', 'blk'), may hold values from 0 to 127
- send_count: int32 [16, 2, 16], P('wide', 'blk'), may hold values from 0 to 24, as said below
- corner_slot: int32 [16, 2, 3, 256], P('wide', 'blk'), may hold values from 0 to 383, as said below
- edge_weight: float32 [16, 2, 3, 256], P('wide', 'blk'), may hold values from 0.2 to 2
Outputs:
- potential: float32 [12, 4096], P(None, ('wide', 'blk'))
Inputs may be any that keep to these rules, and one draw needn't show every extreme that they name: `position`: each column is a unit vector. `slot_vertex`: slots of a block at or beyond the matching send_count are padding and hold arbitrary numbers. send_count[p, b, q] is how many leading slots of block [p, b, q] are live. It is nonzero exactly when (q - p) mod 16 is one of 0, 1, 2, 8, 15, 14, and then at least 12; every owner keeps all 24 slots live for one of the five requesters with (q - p) mod 16 among 0, 1, 2, 15, 14. `corner_slot`: A value c of requester (q, b) names slot c % 24 of owner (c // 24, b); it is always a live slot, and every live slot is named by some corner.
All inputs are finite; a program needn't handle non-finite values.
Results may differ from a plain program's by a relative error of at most 0.0003.
Values sent between devices are 32-bit elements; how exact they have to be, the bound alone decides.
A program may use at most 64 MiB of HBM per device.

v0:
```python
import math

import jax
import jax.numpy as jnp
from jax import lax
from jax.sharding import PartitionSpec as P

stiff_coef = 0.1
source_block = 2048


def shifted(block, axis, distance):
    devices = range(lax.axis_size(axis))
    route = [((i - distance) % len(devices), i) for i in devices]
    return lax.ppermute(block, axis, route)


def kernel_sum(targets, sources, weights, soften):
    number = sources.shape[1]
    block_len = math.gcd(number, source_block)

    def add_block(block_id, running):
        first_col = block_id * block_len
        source_pos = lax.dynamic_slice_in_dim(sources, first_col, block_len, 1)
        source_mass = lax.dynamic_slice_in_dim(weights, first_col, block_len, 1)
        distance = (targets[0][:, None] - source_pos[0][None, :]) ** 2
        distance = distance + (targets[1][:, None] - source_pos[1][None, :]) ** 2
        distance = distance + (targets[2][:, None] - source_pos[2][None, :]) ** 2
        kernel = jnp.log(distance + soften)
        return running + jnp.einsum(
            "fs,ts->ft", source_mass, kernel, precision=lax.Precision.HIGHEST
        )

    start_sum = jnp.zeros((weights.shape[0], targets.shape[1]), jnp.float32)
    return lax.fori_loop(0, number // block_len, add_block, start_sum)


def corner_terms(values, weights):
    value_a, value_b, value_c = (values[..., 0, :], values[..., 1, :], values[..., 2, :])
    weight_a, weight_b, weight_c = (weights[..., 0, :], weights[..., 1, :], weights[..., 2, :])
    term_a = weight_c * (value_a - value_b) + weight_b * (value_a - value_c)
    term_b = weight_c * (value_b - value_a) + weight_a * (value_b - value_c)
    term_c = weight_b * (value_c - value_a) + weight_a * (value_c - value_b)
    return jnp.stack([term_a, term_b, term_c], axis=-2)


def gather_sources(position, masses):
    return lax.all_gather(jnp.concatenate([position, masses], axis=0), "wide", axis=1, tiled=True)


def per_device(position, order_field, cell_area, slot_vertex, send_count, corner_slot, edge_weight):
    fields = order_field.shape[0]
    local_count = order_field.shape[1]
    blk_size = lax.axis_size("blk")
    all_verts = local_count * lax.axis_size("wide") * blk_size
    soften = 4.0 / all_verts
    strength = all_verts ** (-0.5)
    weighted, area_total = lax.psum(
        (jnp.sum(cell_area[None, :] * order_field, axis=1), jnp.sum(cell_area)), ("wide", "blk")
    )
    average = weighted / area_total
    masses = cell_area[None, :] * (order_field - average[:, None])
    pooled = gather_sources(position, masses)
    half_count = local_count // 2
    empty_sum = jnp.zeros((fields, half_count), jnp.float32)

    def turn_pair(turn_id, state_pair):
        upper_half, lower_half = state_pair
        targets = jnp.concatenate([upper_half[:3], lower_half[:3]], axis=1)
        increment = kernel_sum(targets, pooled[:3], pooled[3:], soften)
        upper_half = jnp.concatenate(
            [upper_half[:3], upper_half[3:] + increment[:, :half_count]], axis=0
        )
        lower_half = jnp.concatenate(
            [lower_half[:3], lower_half[3:] + increment[:, half_count:]], axis=0
        )
        upper_half = shifted(upper_half, "blk", 1)
        lower_half = shifted(lower_half, "blk", -1)
        return (upper_half, lower_half)

    start_pair = (
        jnp.concatenate([position[:, :half_count], empty_sum], axis=0),
        jnp.concatenate([position[:, half_count:], empty_sum], axis=0),
    )
    upper_half, lower_half = lax.fori_loop(0, blk_size, turn_pair, start_pair)
    summed = jnp.concatenate([upper_half[3:], lower_half[3:]], axis=1)
    long_range = -strength * summed
    owners = slot_vertex.shape[2]
    slot_len = slot_vertex.shape[3]
    slot_table = slot_vertex.reshape(owners, slot_len)
    live_slot = lax.broadcasted_iota(jnp.int32, (owners, slot_len), 1) < send_count.reshape(
        owners, 1
    )
    safe_slot = jnp.where(live_slot, slot_table, 0)
    outgoing = jnp.where(live_slot[None], order_field[:, safe_slot], 0.0)
    received = lax.all_to_all(outgoing, "wide", split_axis=1, concat_axis=1, tiled=True)
    flat_values = received.reshape(fields, owners * slot_len)
    corners = corner_slot.reshape(3, -1)
    picked = flat_values[:, corners]
    corner_sum = corner_terms(picked, edge_weight.reshape(3, -1))
    returned = (
        jnp.zeros((fields, owners * slot_len), jnp.float32)
        .at[:, corners.reshape(-1)]
        .add(corner_sum.reshape(fields, -1))
        .reshape(fields, owners, slot_len)
    )
    incoming = lax.all_to_all(returned, "wide", split_axis=1, concat_axis=1, tiled=True)
    masked = jnp.where(live_slot[None], incoming, 0.0)
    stiffness = (
        jnp.zeros((fields, local_count), jnp.float32)
        .at[:, safe_slot.reshape(-1)]
        .add(masked.reshape(fields, -1))
    )
    return order_field**3 - order_field + stiff_coef * stiffness / cell_area[None, :] + long_range


def solution(mesh):
    placed = (
        P(None, ("wide", "blk")),
        P(None, ("wide", "blk")),
        P(("wide", "blk")),
        P("wide", "blk", None, None),
        P("wide", "blk", None),
        P("wide", "blk", None, None),
        P("wide", "blk", None, None),
    )
    return jax.shard_map(
        per_device, mesh=mesh, in_specs=placed, out_specs=P(None, ("wide", "blk")), check_vma=False
    )
```

profile of v0, /device:TPU:0, one launch (start us, length us, event | category | flops | bytes accessed | tf_op | source)
XLA Modules:
  0.0 108.8 jit_solution(8041242663535604738)
XLA Ops:
  0.0 0.7 copy-done.6
  0.7 0.8 compare_select_fusion
  1.6 0.6 copy-done
  2.3 1.1 %gather_fusion = f32[384,12]{1,0:T(8,128)S(1)} fusion(f32[12,128]{0,1:T(8,128)S(1)} %copy.57, s32[1024]{0:T(1024)S(1)} %pad_clamp_fusion.1), kind=kCustom, calls=%fused_computation | custom fusion | bytes 38400 | tf_op jit(solution)/shard_map/gather | solution.py:95
  3.6 0.7 reshape.288
  4.3 7.4 %all-to-all-start = ((f32[16,1,288]{2,1,0:T(1,128)}), f32[16,1,288]{2,1,0:T(1,128)S(1)}, u32[]{:S(2)}, u32[]{:S(2)}) async-start(f32[16,1,288]{2,1,0:T(1,128)} %reshape.288), calls=%async_computation | async-start | bytes 49152 | tf_op jit(solution)/shard_map/all_to_all | solution.py:96
  11.9 0.6 copy-done.3
  12.5 0.7 copy-done.5
  13.3 0.6 reduce_sum.19
  14.0 40.9 %all-reduce.2 = (f32[12]{0:T(128)S(1)}, f32[]{:T(128)}) all-reduce(f32[12]{0:T(128)S(1)} %multiply_reduce_fusion, f32[]{:T(128)} %reduce_sum.19), channel_id=1, replica_groups=mesh['wide'=16,'blk'=2] {'wide','blk'}, use_global_device_ids=true, to_apply=%region_3.0 | all-reduce | flops 13 | bytes 104 | tf_op jit(solution)/shard_map/psum | solution.py:58
  54.9 0.7 broadcast_divide_fusion
  55.8 21.7 %all_gather.3 = f32[15,2048]{1,0:T(8,128)S(1)} all-gather(f32[15,128]{1,0:T(8,128)S(1)} %pad_maximum_fusion.4), channel_id=1, replica_groups=mesh['wide'=16,'blk'=2] {'wide'}, dimensions={1}, use_global_device_ids=true | all-gather | bytes 130560 | tf_op jit(solution)/shard_map/all_gather | solution.py:48
  77.5 0.5 broadcast.158
  78.0 0.7 reduce.6
  79.0 1.6 %gather_fusion.1 = f32[768,12]{1,0:T(8,128)S(1)} fusion(f32[12,384]{0,1:T(8,128)S(1)} %bitcast.57, s32[1024]{0:T(1024)S(1)} %pad_clamp_fusion), kind=kCustom, calls=%fused_computation.1 | custom fusion | bytes 76800 | tf_op jit(solution)/shard_map/gather | solution.py:99
  81.0 6.1 %scatter_custom_fusion = f32[12,384]{0,1:T(8,128)S(1)} fusion(s32[768]{0:T(1024)S(1)} %fusion.25, f32[768,12]{1,0:T(8,128)S(1)} %copy.62, f32[]{:T(128)} %constant.12.clone.1), kind=kCustom, calls=%fused_computation.33 | custom fusion | flops 9216 | bytes 18436 | tf_op jit(solution)/shard_map/scatter-add | solution.py:104
  87.3 0.7 reshape.290
  88.0 3.5 %all-to-all-start.1 = ((f32[16,1,288]{2,1,0:T(1,128)}), f32[16,1,288]{2,1,0:T(1,128)S(1)}, u32[]{:S(2)}, u32[]{:S(2)}) async-start(f32[16,1,288]{2,1,0:T(1,128)} %reshape.290), calls=%async_computation.1 | async-start | bytes 49152 | tf_op jit(solution)/shard_map/all_to_all | solution.py:107
  91.5 12.6 %while.12 = (s32[]{:T(128)}, f32[15,64]{1,0:T(8,128)S(1)}, f32[15,64]{1,0:T(8,128)S(1)}, f32[15,2048]{1,0:T(8,128)S(1)}, s32[]{:T(128)}) while((s32[]{:T(128)}, f32[15,64]{1,0:T(8,128)S(1)}, f32[15,64]{1,0:T(8,128)S(1)}, f32[15,2048]{1,0:T(8,128)S(1)}, s32[]{:T(128)}) %tuple.37), condition=%wide.region_7.0_spmd, body=%wide.region_6.7_spmd.sunk | while | flops 40111872 | bytes 278157 | solution.py:85
  91.6 1.3 %convolution_bitcast_fusion.2 = f32[12,128]{1,0:T(8,128)S(1)} fusion(f32[2048]{0:T(1024)S(1)} %bitcast.65, f32[128]{0:T(128)S(1)} %get-tuple-element.112, f32[2048]{0:T(1024)S(1)} %bitcast.66, f32[128]{0:T(128)S(1)} %get-tuple-element.114, f32[2048]{0:T(1024)S(1)} %bitcast.64, f32[128]{0:T(128)S(1)} %get-tuple-element.116, ...), kind=kOutput, calls=%fused_computation.4.clone.1 | convolution fusion | flops 40108032 | bytes 155136 | tf_op jit(solution)/shard_map/while/body/eval_jaxpr/while/body/eval_jaxpr/fs,ts->ft/dot_general | solution.py:30
  93.1 0.6 collective-permute-start.1
  93.6 1.5 %collective-permute-start = (f32[15,64]{1,0:T(8,128)S(1)}, f32[15,64]{1,0:T(8,128)S(1)}, u32[]{:S(2)}, u32[]{:S(2)}) collective-permute-start(f32[15,64]{1,0:T(8,128)S(1)} %pad_maximum_fusion.9), channel_id=1, source_target_pairs={{1,0},{0,1},{3,2},{2,3},{5,4},{4,5},{7,6},{6,7},{9,8},{8,9},{11,10... | collective-permute-start | bytes 11528 | tf_op jit(solution)/shard_map/while/body/eval_jaxpr/ppermute | solution.py:15
  95.2 1.6 %collective-permute-done.1 = f32[15,64]{1,0:T(8,128)S(1)} collective-permute-done((f32[15,64]{1,0:T(8,128)S(1)}, f32[15,64]{1,0:T(8,128)S(1)}, u32[]{:S(2)}, u32[]{:S(2)}) %collective-permute-start.1) | collective-permute-done | bytes 3872 | tf_op jit(solution)/shard_map/while/body/eval_jaxpr/ppermute | solution.py:15
  96.8 0.5 collective-permute-done
  97.4 1.3 %convolution_bitcast_fusion.2 = f32[12,128]{1,0:T(8,128)S(1)} fusion(f32[2048]{0:T(1024)S(1)} %bitcast.65, f32[128]{0:T(128)S(1)} %get-tuple-element.112, f32[2048]{0:T(1024)S(1)} %bitcast.66, f32[128]{0:T(128)S(1)} %get-tuple-element.114, f32[2048]{0:T(1024)S(1)} %bitcast.64, f32[128]{0:T(128)S(1)} %get-tuple-element.116, ...), kind=kOutput, calls=%fused_computation.4.clone.1 | convolution fusion | flops 40108032 | bytes 155136 | tf_op jit(solution)/shard_map/while/body/eval_jaxpr/while/body/eval_jaxpr/fs,ts->ft/dot_general | solution.py:30
  98.8 1.6 %collective-permute-start.1 = (f32[15,64]{1,0:T(8,128)S(1)}, f32[15,64]{1,0:T(8,128)S(1)}, u32[]{:S(2)}, u32[]{:S(2)}) collective-permute-start(f32[15,64]{1,0:T(8,128)S(1)} %pad_maximum_fusion.10), channel_id=1, source_target_pairs={{1,0},{0,1},{3,2},{2,3},{5,4},{4,5},{7,6},{6,7},{9,8},{8,9},{11,10... | collective-permute-start | bytes 11528 | tf_op jit(solution)/shard_map/while/body/eval_jaxpr/ppermute | solution.py:15
  100.4 0.5 collective-permute-start
  100.9 1.6 %collective-permute-done.1 = f32[15,64]{1,0:T(8,128)S(1)} collective-permute-done((f32[15,64]{1,0:T(8,128)S(1)}, f32[15,64]{1,0:T(8,128)S(1)}, u32[]{:S(2)}, u32[]{:S(2)}) %collective-permute-start.1) | collective-permute-done | bytes 3872 | tf_op jit(solution)/shard_map/while/body/eval_jaxpr/ppermute | solution.py:15
  102.5 1.5 %collective-permute-done = f32[15,64]{1,0:T(8,128)S(1)} collective-permute-done((f32[15,64]{1,0:T(8,128)S(1)}, f32[15,64]{1,0:T(8,128)S(1)}, u32[]{:S(2)}, u32[]{:S(2)}) %collective-permute-start) | collective-permute-done | bytes 3872 | tf_op jit(solution)/shard_map/while/body/eval_jaxpr/ppermute | solution.py:15
  104.1 0.7 reduce.7
  105.2 2.8 %scatter_custom_fusion.1 = f32[12,128]{0,1:T(8,128)S(1)} fusion(s32[384]{0:T(512)S(1)} %fusion.27, f32[384,12]{1,0:T(8,128)S(1)} %copy.65, f32[]{:T(128)} %constant.12.clone.1), kind=kCustom, calls=%fused_computation.37 | custom fusion | flops 4608 | bytes 6148 | tf_op jit(solution)/shard_map/scatter-add | solution.py:112
  108.1 0.7 fusion.24
  (66 shorter events, 2.7 us)
Async XLA Ops:
  0.0 0.7 copy-start.6
  1.5 0.7 copy-start
  4.3 73.1 %all-to-all-start = ((f32[16,1,288]{2,1,0:T(1,128)}), f32[16,1,288]{2,1,0:T(1,128)S(1)}, u32[]{:S(2)}, u32[]{:S(2)}) async-start(f32[16,1,288]{2,1,0:T(1,128)} %reshape.288), calls=%async_computation | async-start | bytes 49152 | tf_op jit(solution)/shard_map/all_to_all | solution.py:96
  11.8 0.7 copy-start.3
  12.5 0.7 copy-start.4
  12.5 0.7 copy-start.5
  13.2 0.7 copy-start.1
  54.9 0.7 copy-start.2
  88.0 16.1 %all-to-all-start.1 = ((f32[16,1,288]{2,1,0:T(1,128)}), f32[16,1,288]{2,1,0:T(1,128)S(1)}, u32[]{:S(2)}, u32[]{:S(2)}) async-start(f32[16,1,288]{2,1,0:T(1,128)} %reshape.290), calls=%async_computation.1 | async-start | bytes 49152 | tf_op jit(solution)/shard_map/all_to_all | solution.py:107
  93.1 3.7 %collective-permute-start.1 = (f32[15,64]{1,0:T(8,128)S(1)}, f32[15,64]{1,0:T(8,128)S(1)}, u32[]{:S(2)}, u32[]{:S(2)}) collective-permute-start(f32[15,64]{1,0:T(8,128)S(1)} %pad_maximum_fusion.10), channel_id=1, source_target_pairs={{1,0},{0,1},{3,2},{2,3},{5,4},{4,5},{7,6},{6,7},{9,8},{8,9},{11,10... | collective-permute-start | bytes 11528 | tf_op jit(solution)/shard_map/while/body/eval_jaxpr/ppermute | solution.py:15
  93.6 3.7 %collective-permute-start = (f32[15,64]{1,0:T(8,128)S(1)}, f32[15,64]{1,0:T(8,128)S(1)}, u32[]{:S(2)}, u32[]{:S(2)}) collective-permute-start(f32[15,64]{1,0:T(8,128)S(1)} %pad_maximum_fusion.9), channel_id=1, source_target_pairs={{1,0},{0,1},{3,2},{2,3},{5,4},{4,5},{7,6},{6,7},{9,8},{8,9},{11,10... | collective-permute-start | bytes 11528 | tf_op jit(solution)/shard_map/while/body/eval_jaxpr/ppermute | solution.py:15
  98.8 3.7 %collective-permute-start.1 = (f32[15,64]{1,0:T(8,128)S(1)}, f32[15,64]{1,0:T(8,128)S(1)}, u32[]{:S(2)}, u32[]{:S(2)}) collective-permute-start(f32[15,64]{1,0:T(8,128)S(1)} %pad_maximum_fusion.10), channel_id=1, source_target_pairs={{1,0},{0,1},{3,2},{2,3},{5,4},{4,5},{7,6},{6,7},{9,8},{8,9},{11,10... | collective-permute-start | bytes 11528 | tf_op jit(solution)/shard_map/while/body/eval_jaxpr/ppermute | solution.py:15
  100.4 3.7 %collective-permute-start = (f32[15,64]{1,0:T(8,128)S(1)}, f32[15,64]{1,0:T(8,128)S(1)}, u32[]{:S(2)}, u32[]{:S(2)}) collective-permute-start(f32[15,64]{1,0:T(8,128)S(1)} %pad_maximum_fusion.9), channel_id=1, source_target_pairs={{1,0},{0,1},{3,2},{2,3},{5,4},{4,5},{7,6},{6,7},{9,8},{8,9},{11,10... | collective-permute-start | bytes 11528 | tf_op jit(solution)/shard_map/while/body/eval_jaxpr/ppermute | solution.py:15
where the time goes:
time: 109 us
  blocking collectives  62.6 us (57%)
  starting transfers between devices  15.1 us (14%)
  other arithmetic  13.8 us (13%)
  local copies, waits for them, and re-layouts  9.1 us (8%)
  waiting for transfers between devices  5.28 us (5%)
  matrix products  2.63 us (2%)
    psum x1, blocking collectives, per_device(): lax.psum((jnp.sum(cell_area[None, :] * order_field, axis=1), jnp.sum(cell...  40.9 us
    all_gather x1, blocking collectives, gather_sources(): lax.all_gather(jnp.concatenate([position, masses], axis=0), 'wide', axis=...  21.7 us
    all_to_all x1, starting transfers between devices, per_device(): lax.all_to_all(outgoing, 'wide', split_axis=1, concat_axis=1, tiled=True)  7.41 us
    scatter-add x1, other arithmetic, per_device(): returned = jnp.zeros((fields, owners * slot_len), jnp.float32).at[:, corn...  6.08 us
    ppermute x4, waiting for transfers between devices, shifted(): return lax.ppermute(block, axis, route)  5.27 us
    unnamed x21, local copies, waits for them, and re-layouts  4.29 us
    ppermute x4, starting transfers between devices, shifted(): return lax.ppermute(block, axis, route)  4.18 us
    all_to_all x1, starting transfers between devices, per_device(): lax.all_to_all(returned, 'wide', split_axis=1, concat_axis=1, tiled=True)  3.49 us
  transfers between devices with their start and end apart: 6, of which 4 were waited for; matrix products, arithmetic and copies ran while one was open for 4% of the time, Pallas kernels for 0%

commit v1 on v0

v1 whole, which is shorter than its diff:
```python
import functools

import jax
import jax.numpy as jnp
from jax import lax
from jax.experimental import pallas as pl
from jax.experimental.pallas import tpu as pltpu
from jax.sharding import PartitionSpec as P

stiff_coef = 0.1
LANES = 128
GROUP = 4
MESH = pl.DeviceIdType.MESH
NT = (((1,), (1,)), ((), ()))
NN = (((1,), (0,)), ((), ()))


def halves(x):
    hi = x.astype(jnp.bfloat16)
    lo = (x - hi.astype(jnp.float32)).astype(jnp.bfloat16)
    return hi, lo


def stacked(x):
    return jnp.concatenate(halves(x), axis=0)


def mm(a, b, dims):
    return lax.dot_general(a, b, dims, preferred_element_type=jnp.float32)


def kernel(
    wide, blk, fields, slot_len,
    pos_ref, order_ref, area_ref, slot_ref, count_ref, corner_ref, weight_ref,
    out_ref,
    blocks, vout, vbuf, rout, rbuf, targets, acc_ref, sum_ref,
    bsend, brecv, vsend, vrecv, rsend, rrecv,
):
    n = wide * blk
    my_w, my_b = lax.axis_index("wide"), lax.axis_index("blk")
    me = my_w * blk + my_b
    rows = fields + 4
    soften = 4.0 / (n * LANES)
    strength = float(n * LANES) ** (-0.5)
    offsets = (1, wide - 1, 2, wide - 2, wide // 2)

    def device(step):
        to = lax.rem(me + step, n)
        return (to // blk, lax.rem(to, blk))

    barrier = pltpu.get_barrier_semaphore()

    def greet(step, carry):
        pl.semaphore_signal(barrier, inc=1, device_id=device(step), device_id_type=MESH)
        return carry

    lax.fori_loop(1, n, greet, 0)

    blocks[0, :fields] = order_ref[...]
    blocks[0, fields:fields + 3] = pos_ref[...]
    blocks[0, fields + 3:] = area_ref[...]
    own = jnp.concatenate([order_ref[...], pos_ref[...], area_ref[...]], axis=0)
    area = area_ref[...]

    lane = lax.broadcasted_iota(jnp.int32, (1, 2 * LANES), 1)
    base = jnp.full((1, 2 * LANES), -1, jnp.int32)
    towards = jnp.full((1, 2 * LANES), -1, jnp.int32)
    for k, offset in enumerate(offsets + (0,)):
        first = k * slot_len if offset else LANES
        inside = (lane >= first) & (lane < first + slot_len)
        base = jnp.where(inside, lane - first, base)
        towards = jnp.where(inside, lax.rem(my_w + offset, wide), towards)
    count_lane = lax.broadcasted_iota(jnp.int32, (wide, wide), 1)
    count_row = lax.broadcasted_iota(jnp.int32, (wide, wide), 0)
    counts = count_ref[0].astype(jnp.float32)
    counts = jnp.sum(jnp.where(count_lane == count_row, counts, 0.0), axis=1, keepdims=True)
    slot_id = lax.broadcasted_iota(jnp.int32, (wide, slot_len), 1).astype(jnp.float32)
    table = jnp.where(slot_id < counts, slot_ref[0, 0].astype(jnp.float32) + 1.0, 0.0)
    spread_row = lax.broadcasted_iota(jnp.int32, (slot_len, 2 * LANES), 0)
    spread = jnp.where(spread_row == base, 1.0, 0.0).astype(jnp.bfloat16)
    spread_table = mm(table.astype(jnp.bfloat16), spread, NN)
    wide_row = lax.broadcasted_iota(jnp.int32, (wide, 2 * LANES), 0)
    vertex_of = jnp.sum(jnp.where(wide_row == towards, spread_table, 0.0), axis=0, keepdims=True)
    vertex_row = lax.broadcasted_iota(jnp.int32, (LANES, 2 * LANES), 0).astype(jnp.float32) + 1.0
    place = jnp.where(vertex_row == vertex_of, 1.0, 0.0).astype(jnp.bfloat16)
    outgoing = mm(stacked(own), place, NN)
    outgoing = outgoing[:rows] + outgoing[rows:]
    vout[...] = outgoing[:, :LANES]
    own_values = outgoing[:, LANES:]

    columns = own.T
    for k in range(3):
        targets[k] = jnp.broadcast_to(columns[:, fields + k:fields + k + 1], (LANES, LANES))
    row_id = lax.broadcasted_iota(jnp.int32, (rows, 1), 0)
    center = jnp.sum(own * area, axis=1, keepdims=True) / jnp.sum(area)
    center = jnp.where(row_id < fields, center, 0.0)

    pl.semaphore_wait(barrier, n - 1)

    def value_copy(k):
        return pltpu.make_async_remote_copy(
            src_ref=vout, dst_ref=vbuf.at[k], send_sem=vsend.at[k], recv_sem=vrecv.at[k],
            device_id=(lax.rem(my_w + offsets[k], wide), my_b), device_id_type=MESH,
        )

    def term_copy(k):
        return pltpu.make_async_remote_copy(
            src_ref=rout, dst_ref=rbuf.at[k], send_sem=rsend.at[k], recv_sem=rrecv.at[k],
            device_id=(lax.rem(my_w + wide - offsets[k], wide), my_b), device_id_type=MESH,
        )

    def block_copy(step):
        return pltpu.make_async_remote_copy(
            src_ref=blocks.at[0], dst_ref=blocks.at[step], send_sem=bsend.at[step],
            recv_sem=brecv.at[step], device_id=device(step), device_id_type=MESH,
        )

    for k in range(5):
        value_copy(k).start()

    def start_block(step, carry):
        block_copy(step).start()
        return carry

    lax.fori_loop(1, n, start_block, 0)

    corner_rows = []
    for c in range(3):
        corner = corner_ref[0, 0, c:c + 1, :]
        column = jnp.full(corner.shape, -1, jnp.int32)
        for k, offset in enumerate(offsets + (0,)):
            low = lax.rem(my_w + wide - offset, wide) * slot_len
            first = k * slot_len if offset else LANES
            column = jnp.where((corner >= low) & (corner < low + slot_len), corner - low + first, column)
        corner_rows.append(column)
    elements = corner_rows[0].shape[1]
    column = jnp.concatenate(corner_rows, axis=1)
    column_id = lax.broadcasted_iota(jnp.int32, (2 * LANES, 3 * elements), 0)
    pick = jnp.where(column_id == column, 1.0, 0.0).astype(jnp.bfloat16)

    part_lane = lax.broadcasted_iota(jnp.int32, (1, LANES), 1)

    def merged(buffer):
        total = jnp.zeros((rows, LANES), jnp.float32)
        for k in range(5):
            inside = (part_lane >= k * slot_len) & (part_lane < (k + 1) * slot_len)
            total = jnp.where(inside, buffer[k], total)
        return total

    for k in range(5):
        value_copy(k).wait_recv()
    values = jnp.concatenate([merged(vbuf), own_values], axis=1)
    picked = mm(stacked(values), pick, NN)
    picked = picked[:rows] + picked[rows:]
    value_a, value_b, value_c = (picked[:, c * elements:(c + 1) * elements] for c in range(3))
    weight_a, weight_b, weight_c = (weight_ref[0, 0, c:c + 1, :] for c in range(3))
    along_ab = weight_c * (value_a - value_b)
    along_ac = weight_b * (value_a - value_c)
    along_bc = weight_a * (value_b - value_c)
    terms = jnp.concatenate(
        [along_ab + along_ac, along_bc - along_ab, -along_ac - along_bc], axis=1
    )
    returned = mm(stacked(terms), pick, NT)
    returned = returned[:rows] + returned[rows:]
    rout[...] = returned[:, :LANES]
    own_terms = returned[:, LANES:]

    factor_row = row_id < fields

    def add_group(first, acc, sums):
        his, los, weights = [], [], []
        for u in range(GROUP):
            block = blocks[first + u]
            distance = (targets[0] - block[fields:fields + 1]) ** 2
            distance = distance + (targets[1] - block[fields + 1:fields + 2]) ** 2
            distance = distance + (targets[2] - block[fields + 2:fields + 3]) ** 2
            hi, lo = halves(jnp.log(distance + soften))
            mass = (block - center) * jnp.where(factor_row, block[fields + 3:], 1.0)
            sums = sums + mass
            his.append(hi)
            los.append(lo)
            weights.append(stacked(mass))
        weight = jnp.concatenate(weights, axis=1)
        acc = acc + mm(jnp.concatenate(his, axis=1), weight, NT)
        acc = acc + mm(jnp.concatenate(los, axis=1), weight, NT)
        return acc, sums

    for step in range(1, GROUP):
        block_copy(step).wait_recv()
    acc, sums = add_group(
        0, jnp.zeros((LANES, 2 * rows), jnp.float32), jnp.zeros((rows, LANES), jnp.float32)
    )

    for k in range(5):
        term_copy(k).start()

    def one_group(group, carry):
        first = group * GROUP
        for u in range(GROUP):
            block_copy(first + u).wait_recv()
        return add_group(first, *carry)

    acc, sums = lax.fori_loop(1, n // GROUP, one_group, (acc, sums))
    total = acc.T
    total = total[:rows] + total[rows:]
    sums = jnp.sum(sums, axis=1, keepdims=True)
    shift = sums / sums[fields + 3:]
    long_range = -strength * (total - shift * total[fields + 3:])

    for k in range(5):
        term_copy(k).wait_recv()
    back = jnp.concatenate([merged(rbuf), own_terms], axis=1)
    stiffness = mm(stacked(back), place, NT)
    stiffness = stiffness[:rows] + stiffness[rows:]
    result = stiff_coef * stiffness / area + long_range
    out_ref[...] = result[:fields]

    def sent(step, carry):
        block_copy(step).wait_send()
        return carry

    lax.fori_loop(1, n, sent, 0)
    for k in range(5):
        value_copy(k).wait_send()
        term_copy(k).wait_send()


def per_device(position, order_field, cell_area, slot_vertex, send_count, corner_slot, edge_weight):
    fields, local_count = order_field.shape
    wide, blk = lax.axis_size("wide"), lax.axis_size("blk")
    n = wide * blk
    rows = fields + 4
    slot_len = slot_vertex.shape[3]
    vmem = pl.BlockSpec(memory_space=pltpu.VMEM)
    dma = pltpu.SemaphoreType.DMA
    extra = pl.pallas_call(
        functools.partial(kernel, wide, blk, fields, slot_len),
        out_shape=jax.ShapeDtypeStruct((fields, local_count), jnp.float32),
        in_specs=[vmem] * 7,
        out_specs=vmem,
        scratch_shapes=[
            pltpu.VMEM((n, rows, LANES), jnp.float32),
            pltpu.VMEM((rows, LANES), jnp.float32),
            pltpu.VMEM((5, rows, LANES), jnp.float32),
            pltpu.VMEM((rows, LANES), jnp.float32),
            pltpu.VMEM((5, rows, LANES), jnp.float32),
            pltpu.VMEM((3, LANES, LANES), jnp.float32),
            pltpu.VMEM((LANES, 2 * rows), jnp.float32),
            pltpu.VMEM((rows, LANES), jnp.float32),
            dma((n,)), dma((n,)), dma((5,)), dma((5,)), dma((5,)), dma((5,)),
        ],
        compiler_params=pltpu.CompilerParams(collective_id=0, has_side_effects=True),
    )(position, order_field, cell_area.reshape(1, local_count), slot_vertex, send_count,
      corner_slot, edge_weight)
    return order_field**3 - order_field + extra


def solution(mesh):
    placed = (
        P(None, ("wide", "blk")),
        P(None, ("wide", "blk")),
        P(("wide", "blk")),
        P("wide", "blk", None, None),
        P("wide", "blk", None),
        P("wide", "blk", None, None),
        P("wide", "blk", None, None),
    )
    return jax.shard_map(
        per_device, mesh=mesh, in_specs=placed, out_specs=P(None, ("wide", "blk")), check_vma=False
    )
```

time: 109 us -> 21.8 us (0.20)
  blocking collectives: 62.6 us -> 0 us
  Pallas kernels: 0 us -> 18.3 us
  starting transfers between devices: 15.1 us -> 0 us
  other arithmetic: 13.8 us -> 1.3 us
  local copies, waits for them, and re-layouts: 9.1 us -> 1.89 us
  waiting for transfers between devices: 5.28 us -> 0 us
  matrix products: 2.63 us -> 0 us
    psum x1 -> x0, blocking collectives: 40.9 us -> none  [per_device(): lax.psum((jnp.sum(cell_area[None, :] * order_field, axis=1), jnp.sum(cell...]
    all_gather x1 -> x0, blocking collectives: 21.7 us -> none  [gather_sources(): lax.all_gather(jnp.concatenate([position, masses], axis=0), 'wide', axis=...]
    pallas_call x0 -> x1, Pallas kernels: none -> 18.3 us  [per_device(): pl.pallas_call(functools.partial(kernel, wide, blk, fields, slot_len), ou...]
    all_to_all x2 -> x0, starting transfers between devices: 10.9 us -> none  [the longest x1 7.41 us: per_device(): lax.all_to_all(outgoing, 'wide', split_axis=1, concat_axis=1, tiled=True)]
    scatter-add x2 -> x0, other arithmetic: 8.87 us -> none  [the longest x1 6.08 us: per_device(): returned = jnp.zeros((fields, owners * slot_len), jnp.float32).at[:, corn...]
    ppermute x4 -> x0, waiting for transfers between devices: 5.27 us -> none  [shifted(): return lax.ppermute(block, axis, route)]
    ppermute x4 -> x0, starting transfers between devices: 4.18 us -> none  [shifted(): return lax.ppermute(block, axis, route)]
    gather x4 -> x0, local copies, waits for them, and re-layouts: 2.99 us -> none  [the longest x2 1.72 us: per_device(): picked = flat_values[:, corners]]
  transfers between devices with their start and end apart: 6 -> 0, of which waited for: 4 -> 0; matrix products, arithmetic and copies ran while one was open for 4% -> 0% of each run, Pallas kernels for 0% -> 0%
where the time goes in v1:
time: 21.8 us; the launch traced here: 21.5 us
  Pallas kernels  18.3 us (84%)
  local copies, waits for them, and re-layouts  1.89 us (9%)
  other arithmetic  1.3 us (6%)
    pallas_call x1, Pallas kernels, per_device(): pl.pallas_call(functools.partial(kernel, wide, blk, fields, slot_len), ou...  18.3 us
    unnamed x6, local copies, waits for them, and re-layouts  1.89 us
    add x1, other arithmetic, per_device(): return order_field ** 3 - order_field + extra  1.3 us

profile of v1, /device:TPU:0, one launch (start us, length us, event | category | flops | bytes accessed | tf_op | source)
XLA Modules:
  0.0 21.5 jit_solution(990371705498498038)
XLA Ops:
  0.0 0.0 copy-start.1
  0.0 1.3 %copy.8.corner_ref = s32[1,1,3,256]{3,2,1,0:T(4,128)} copy(s32[1,1,3,256]{3,1,2,0:T(1,128)} %param.12) | data formatting | bytes 6144 | tf_op args[5]
  1.3 0.0 copy-done.1
  1.3 0.6 %copy.9.weight_ref = f32[1,1,3,256]{3,2,1,0:T(4,128)} copy(f32[1,1,3,256]{3,1,2,0:T(1,128)S(1)} %copy-done.1) | data formatting | bytes 6144 | tf_op args[6]
  1.9 0.0 copy-start
  1.9 18.3 %shard_map.73 = f32[12,128]{1,0:T(8,128)} custom-call(f32[3,128]{1,0:T(4,128)} %pos_ref.1, f32[12,128]{1,0:T(8,128)} %order_ref.1, f32[1,128]{1,0:T(1,128)} %bitcast.1, s32[1,1,16,24]{3,2,1,0:T(8,128)} %slot_ref.1, s32[1,1,16]{2,1,0:T(1,128)} %count_ref.1, s32[1,1,3,256]{3,2,1,0:T(4,128)} %copy.8.corner_ref, f32[1,1,3,256]{3,2,1,0:T(4,128)} %copy.9.weight_ref), custom_call_target="tpu_custom_call" | custom-call | tf_op jit(solution)/shard_map/pallas_call | solution.py:236
  20.2 0.0 copy-done
  20.2 1.3 %fusion = f32[12,128]{1,0:T(8,128)} fusion(f32[12,128]{1,0:T(8,128)} %shard_map.73, f32[12,128]{1,0:T(8,128)S(1)} %copy-done), kind=kLoop, calls=%fused_computation.1 | loop fusion | flops 6144 | bytes 18432 | tf_op jit(solution)/shard_map/add | solution.py:255
Async XLA Ops:
  0.0 1.3 %copy-start.1 = (f32[1,1,3,256]{3,1,2,0:T(1,128)S(1)}, f32[1,1,3,256]{3,1,2,0:T(1,128)}, u32[]{:S(2)}) copy-start(f32[1,1,3,256]{3,1,2,0:T(1,128)} %param.13) | copy-start | bytes 9220
  1.9 18.3 %copy-start = (f32[12,128]{1,0:T(8,128)S(1)}, f32[12,128]{1,0:T(8,128)}, u32[]{:S(2)}) copy-start(f32[12,128]{1,0:T(8,128)} %order_ref.1) | copy-start | bytes 18436

commit v2 on v1

--- a/solution.py
+++ b/solution.py
@@ -31,10 +31,11 @@
 
 def kernel(
     wide, blk, fields, slot_len,
+    pos_hbm, order_hbm, area_hbm, slot_hbm, count_hbm, corner_hbm, weight_hbm,
+    out_ref,
     pos_ref, order_ref, area_ref, slot_ref, count_ref, corner_ref, weight_ref,
-    out_ref,
-    blocks, vout, vbuf, rout, rbuf, targets, acc_ref, sum_ref,
-    bsend, brecv, vsend, vrecv, rsend, rrecv,
+    blocks, vout, vbuf, rout, rbuf, targets,
+    isem, bsend, brecv, vsend, vrecv, rsend, rrecv,
 ):
     n = wide * blk
     my_w, my_b = lax.axis_index("wide"), lax.axis_index("blk")
@@ -48,6 +49,15 @@
         to = lax.rem(me + step, n)
         return (to // blk, lax.rem(to, blk))
 
+    loads = [
+        pltpu.make_async_copy(source, held, isem.at[i])
+        for i, (source, held) in enumerate((
+            (order_hbm, order_ref), (area_hbm, area_ref), (pos_hbm, pos_ref), (slot_hbm, slot_ref),
+            (count_hbm, count_ref), (corner_hbm, corner_ref), (weight_hbm, weight_ref),
+        ))
+    ]
+    for load in loads:
+        load.start()
     barrier = pltpu.get_barrier_semaphore()
 
     def greet(step, carry):
@@ -55,6 +65,8 @@
         return carry
 
     lax.fori_loop(1, n, greet, 0)
+    for load in loads:
+        load.wait()
 
     blocks[0, :fields] = order_ref[...]
     blocks[0, fields:fields + 3] = pos_ref[...]
@@ -95,8 +107,6 @@
     center = jnp.sum(own * area, axis=1, keepdims=True) / jnp.sum(area)
     center = jnp.where(row_id < fields, center, 0.0)
 
-    pl.semaphore_wait(barrier, n - 1)
-
     def value_copy(k):
         return pltpu.make_async_remote_copy(
             src_ref=vout, dst_ref=vbuf.at[k], send_sem=vsend.at[k], recv_sem=vrecv.at[k],
@@ -115,18 +125,9 @@
             recv_sem=brecv.at[step], device_id=device(step), device_id_type=MESH,
         )
 
-    for k in range(5):
-        value_copy(k).start()
-
-    def start_block(step, carry):
-        block_copy(step).start()
-        return carry
-
-    lax.fori_loop(1, n, start_block, 0)
-
     corner_rows = []
     for c in range(3):
-        corner = corner_ref[0, 0, c:c + 1, :]
+        corner = corner_ref[c]
         column = jnp.full(corner.shape, -1, jnp.int32)
         for k, offset in enumerate(offsets + (0,)):
             low = lax.rem(my_w + wide - offset, wide) * slot_len
@@ -138,6 +139,16 @@
     column_id = lax.broadcasted_iota(jnp.int32, (2 * LANES, 3 * elements), 0)
     pick = jnp.where(column_id == column, 1.0, 0.0).astype(jnp.bfloat16)
 
+    pl.semaphore_wait(barrier, n - 1)
+    for k in range(5):
+        value_copy(k).start()
+
+    def start_block(step, carry):
+        block_copy(step).start()
+        return carry
+
+    lax.fori_loop(1, n, start_block, 0)
+
     part_lane = lax.broadcasted_iota(jnp.int32, (1, LANES), 1)
 
     def merged(buffer):
@@ -153,7 +164,7 @@
     picked = mm(stacked(values), pick, NN)
     picked = picked[:rows] + picked[rows:]
     value_a, value_b, value_c = (picked[:, c * elements:(c + 1) * elements] for c in range(3))
-    weight_a, weight_b, weight_c = (weight_ref[0, 0, c:c + 1, :] for c in range(3))
+    weight_a, weight_b, weight_c = (weight_ref[c] for c in range(3))
     along_ab = weight_c * (value_a - value_b)
     along_ac = weight_b * (value_a - value_c)
     along_bc = weight_a * (value_b - value_c)
@@ -231,27 +242,29 @@
     n = wide * blk
     rows = fields + 4
     slot_len = slot_vertex.shape[3]
+    args = (
+        position, order_field, cell_area.reshape(1, local_count), slot_vertex, send_count,
+        corner_slot.reshape(3, 1, -1), edge_weight.reshape(3, 1, -1),
+    )
     vmem = pl.BlockSpec(memory_space=pltpu.VMEM)
     dma = pltpu.SemaphoreType.DMA
     extra = pl.pallas_call(
         functools.partial(kernel, wide, blk, fields, slot_len),
-        out_shape=jax.ShapeDtypeStruct((fields, local_count), jnp.float32),
-        in_specs=[vmem] * 7,
+        out_shape=pltpu.VMEM((fields, local_count), jnp.float32),
+        in_specs=[pl.BlockSpec(memory_space=pl.ANY)] * 7,
         out_specs=vmem,
         scratch_shapes=[
+            *(pltpu.VMEM(x.shape, x.dtype) for x in args),
             pltpu.VMEM((n, rows, LANES), jnp.float32),
             pltpu.VMEM((rows, LANES), jnp.float32),
             pltpu.VMEM((5, rows, LANES), jnp.float32),
             pltpu.VMEM((rows, LANES), jnp.float32),
             pltpu.VMEM((5, rows, LANES), jnp.float32),
             pltpu.VMEM((3, LANES, LANES), jnp.float32),
-            pltpu.VMEM((LANES, 2 * rows), jnp.float32),
-            pltpu.VMEM((rows, LANES), jnp.float32),
-            dma((n,)), dma((n,)), dma((5,)), dma((5,)), dma((5,)), dma((5,)),
+            dma((7,)), dma((n,)), dma((n,)), dma((5,)), dma((5,)), dma((5,)), dma((5,)),
         ],
         compiler_params=pltpu.CompilerParams(collective_id=0, has_side_effects=True),
-    )(position, order_field, cell_area.reshape(1, local_count), slot_vertex, send_count,
-      corner_slot, edge_weight)
+    )(*args)
     return order_field**3 - order_field + extra
 
 

time: 21.8 us -> 17.8 us (0.82)
  local copies, waits for them, and re-layouts: 1.89 us -> 0.01 us
  Pallas kernels: 18.3 us -> 17 us
  other arithmetic: 1.3 us -> 0.6 us
    unnamed x6 -> x2, local copies, waits for them, and re-layouts: 1.89 us -> 0.01 us
    pallas_call x1, Pallas kernels: 18.3 us -> 17 us  [per_device(): pl.pallas_call(functools.partial(kernel, wide, blk, fields, slot_len), ou...]
    add x1, other arithmetic: 1.3 us -> 0.6 us  [per_device(): return order_field ** 3 - order_field + extra]
where the time goes in v2:
time: 17.8 us; the launch traced here: 17.7 us
  Pallas kernels  17 us (96%)
  other arithmetic  0.6 us (3%)
    pallas_call x1, Pallas kernels, per_device(): pl.pallas_call(functools.partial(kernel, wide, blk, fields, slot_len), ou...  17 us
    add x1, other arithmetic, per_device(): return order_field ** 3 - order_field + extra  0.6 us

profile of v2, /device:TPU:0, one launch (start us, length us, event | category | flops | bytes accessed | tf_op | source)
XLA Modules:
  0.0 17.7 jit_solution(13157832612893027887)
XLA Ops:
  0.0 0.0 copy-start
  0.0 17.0 %shard_map.73 = f32[12,128]{1,0:T(8,128)S(1)} custom-call(f32[3,128]{1,0:T(4,128)} %pos_hbm.1, f32[12,128]{1,0:T(8,128)} %order_hbm.1, f32[1,128]{1,0:T(1,128)} %bitcast.5, s32[1,1,16,24]{3,2,1,0:T(8,128)} %slot_hbm.1, s32[1,1,16]{2,1,0:T(1,128)} %count_hbm.1, s32[3,1,256]{2,1,0:T(1,128)} %bitcast.3, f32[3,1,256]{2,1,0:T(1,128)} %bitcast.4), custom_call_target="tpu_custom_call" | custom-call | tf_op jit(solution)/shard_map/pallas_call | solution.py:251
  17.0 0.0 copy-done
  17.1 0.6 %fusion = f32[12,128]{1,0:T(8,128)} fusion(f32[12,128]{1,0:T(8,128)S(1)} %shard_map.73, f32[12,128]{1,0:T(8,128)S(1)} %copy-done), kind=kLoop, calls=%fused_computation.1 | loop fusion | flops 6144 | bytes 18432 | tf_op jit(solution)/shard_map/add | solution.py:268
Async XLA Ops:
  0.0 17.0 %copy-start = (f32[12,128]{1,0:T(8,128)S(1)}, f32[12,128]{1,0:T(8,128)}, u32[]{:S(2)}) copy-start(f32[12,128]{1,0:T(8,128)} %order_hbm.1) | copy-start | bytes 18436

commit v3 on v2

--- a/solution.py
+++ b/solution.py
@@ -9,6 +9,7 @@
 
 stiff_coef = 0.1
 LANES = 128
+PAD = 32
 GROUP = 4
 MESH = pl.DeviceIdType.MESH
 NT = (((1,), (1,)), ((), ()))
@@ -34,8 +35,8 @@
     pos_hbm, order_hbm, area_hbm, slot_hbm, count_hbm, corner_hbm, weight_hbm,
     out_ref,
     pos_ref, order_ref, area_ref, slot_ref, count_ref, corner_ref, weight_ref,
-    blocks, vout, vbuf, rout, rbuf, targets,
-    isem, bsend, brecv, vsend, vrecv, rsend, rrecv,
+    blocks, vout, vbuf, kout, kbuf, targets,
+    isem, bsend, brecv, vsend, vrecv, ksend, krecv,
 ):
     n = wide * blk
     my_w, my_b = lax.axis_index("wide"), lax.axis_index("blk")
@@ -44,6 +45,9 @@
     soften = 4.0 / (n * LANES)
     strength = float(n * LANES) ** (-0.5)
     offsets = (1, wide - 1, 2, wide - 2, wide // 2)
+    around = offsets + (0,)
+    spans = sorted({(p - q) % wide for p in around for q in around} - {0})
+    total_slots = kbuf.shape[0]
 
     def device(step):
         to = lax.rem(me + step, n)
@@ -77,8 +81,9 @@
     lane = lax.broadcasted_iota(jnp.int32, (1, 2 * LANES), 1)
     base = jnp.full((1, 2 * LANES), -1, jnp.int32)
     towards = jnp.full((1, 2 * LANES), -1, jnp.int32)
-    for k, offset in enumerate(offsets + (0,)):
-        first = k * slot_len if offset else LANES
+    places = [(k * slot_len, offset) for k, offset in enumerate(offsets)]
+    places += [(LANES + g * PAD, 0) for g in range(fields // 4)]
+    for first, offset in places:
         inside = (lane >= first) & (lane < first + slot_len)
         base = jnp.where(inside, lane - first, base)
         towards = jnp.where(inside, lax.rem(my_w + offset, wide), towards)
@@ -97,8 +102,13 @@
     place = jnp.where(vertex_row == vertex_of, 1.0, 0.0).astype(jnp.bfloat16)
     outgoing = mm(stacked(own), place, NN)
     outgoing = outgoing[:rows] + outgoing[rows:]
-    vout[...] = outgoing[:, :LANES]
+    part_lane = lax.broadcasted_iota(jnp.int32, (1, LANES), 1)
     own_values = outgoing[:, LANES:]
+    packed = own_values[:4]
+    for g in range(1, fields // 4):
+        packed = jnp.where(part_lane >= g * PAD, own_values[4 * g:4 * g + 4], packed)
+    vout[:fields] = outgoing[:fields, :LANES]
+    vout[fields:] = packed
 
     columns = own.T
     for k in range(3):
@@ -110,12 +120,14 @@
     def value_copy(k):
         return pltpu.make_async_remote_copy(
             src_ref=vout, dst_ref=vbuf.at[k], send_sem=vsend.at[k], recv_sem=vrecv.at[k],
-            device_id=(lax.rem(my_w + offsets[k], wide), my_b), device_id_type=MESH,
+            device_id=(lax.rem(my_w + k, wide), my_b), device_id_type=MESH,
         )
 
-    def term_copy(k):
+    def matrix_copy(k):
+        part = pl.ds(k * slot_len, slot_len)
         return pltpu.make_async_remote_copy(
-            src_ref=rout, dst_ref=rbuf.at[k], send_sem=rsend.at[k], recv_sem=rrecv.at[k],
+            src_ref=kout.at[part], dst_ref=kbuf.at[part], send_sem=ksend.at[k],
+            recv_sem=krecv.at[k],
             device_id=(lax.rem(my_w + wide - offsets[k], wide), my_b), device_id_type=MESH,
         )
 
@@ -134,47 +146,32 @@
             first = k * slot_len if offset else LANES
             column = jnp.where((corner >= low) & (corner < low + slot_len), corner - low + first, column)
         corner_rows.append(column)
-    elements = corner_rows[0].shape[1]
-    column = jnp.concatenate(corner_rows, axis=1)
-    column_id = lax.broadcasted_iota(jnp.int32, (2 * LANES, 3 * elements), 0)
-    pick = jnp.where(column_id == column, 1.0, 0.0).astype(jnp.bfloat16)
+    column_id = lax.broadcasted_iota(jnp.int32, (total_slots, 1), 0)
+    picks = [jnp.where(column_id == column, 1.0, 0.0) for column in corner_rows]
+    signs, heavy, light = [], [], []
+    for c in range(3):
+        edge = picks[(c + 1) % 3] - picks[(c + 2) % 3]
+        hi, lo = (half.astype(jnp.float32) for half in halves(weight_ref[c]))
+        signs.append(edge.astype(jnp.bfloat16))
+        heavy.append((edge * hi).astype(jnp.bfloat16))
+        light.append((edge * lo).astype(jnp.bfloat16))
+    signs = jnp.concatenate(signs, axis=1)
+    matrix = mm(jnp.concatenate(heavy, axis=1), signs, NT)
+    matrix = matrix + mm(jnp.concatenate(light, axis=1), signs, NT)
+    kout[...] = matrix
+    own_matrix = matrix[LANES:]
 
     pl.semaphore_wait(barrier, n - 1)
-    for k in range(5):
-        value_copy(k).start()
-
     def start_block(step, carry):
         block_copy(step).start()
         return carry
 
     lax.fori_loop(1, n, start_block, 0)
 
-    part_lane = lax.broadcasted_iota(jnp.int32, (1, LANES), 1)
-
-    def merged(buffer):
-        total = jnp.zeros((rows, LANES), jnp.float32)
-        for k in range(5):
-            inside = (part_lane >= k * slot_len) & (part_lane < (k + 1) * slot_len)
-            total = jnp.where(inside, buffer[k], total)
-        return total
-
+    for k in spans:
+        value_copy(k).start()
     for k in range(5):
-        value_copy(k).wait_recv()
-    values = jnp.concatenate([merged(vbuf), own_values], axis=1)
-    picked = mm(stacked(values), pick, NN)
-    picked = picked[:rows] + picked[rows:]
-    value_a, value_b, value_c = (picked[:, c * elements:(c + 1) * elements] for c in range(3))
-    weight_a, weight_b, weight_c = (weight_ref[c] for c in range(3))
-    along_ab = weight_c * (value_a - value_b)
-    along_ac = weight_b * (value_a - value_c)
-    along_bc = weight_a * (value_b - value_c)
-    terms = jnp.concatenate(
-        [along_ab + along_ac, along_bc - along_ab, -along_ac - along_bc], axis=1
-    )
-    returned = mm(stacked(terms), pick, NT)
-    returned = returned[:rows] + returned[rows:]
-    rout[...] = returned[:, :LANES]
-    own_terms = returned[:, LANES:]
+        matrix_copy(k).start()
 
     factor_row = row_id < fields
 
@@ -202,9 +199,6 @@
         0, jnp.zeros((LANES, 2 * rows), jnp.float32), jnp.zeros((rows, LANES), jnp.float32)
     )
 
-    for k in range(5):
-        term_copy(k).start()
-
     def one_group(group, carry):
         first = group * GROUP
         for u in range(GROUP):
@@ -218,9 +212,43 @@
     shift = sums / sums[fields + 3:]
     long_range = -strength * (total - shift * total[fields + 3:])
 
+    for k in spans:
+        value_copy(k).wait_recv()
     for k in range(5):
-        term_copy(k).wait_recv()
-    back = jnp.concatenate([merged(rbuf), own_terms], axis=1)
+        matrix_copy(k).wait_recv()
+
+    def sent_values(span):
+        return vout[...] if span == 0 else vbuf[span]
+
+    gathered = []
+    for offset in around:
+        total_values = jnp.zeros((rows, LANES), jnp.float32)
+        for k in range(5):
+            inside = (part_lane >= k * slot_len) & (part_lane < (k + 1) * slot_len)
+            total_values = jnp.where(
+                inside, sent_values((offsets[k] - offset) % wide), total_values
+            )
+        packed = sent_values((-offset) % wide)
+        parts = [
+            (pltpu.roll(packed, LANES - g * PAD, 1) if g else packed)[fields:, :PAD]
+            for g in range(fields // 4)
+        ]
+        parts.append(jnp.zeros((rows - fields, PAD), jnp.float32))
+        gathered.append(
+            jnp.concatenate([total_values, jnp.concatenate(parts, axis=0)], axis=1)
+        )
+    gathered = jnp.concatenate(gathered, axis=0)
+    high, low = halves(gathered)
+    matrix_high, matrix_low = halves(jnp.concatenate([kbuf[:LANES], own_matrix], axis=0))
+    product = mm(jnp.concatenate([high, low], axis=0), matrix_high, NT)
+    product = product[:6 * rows] + product[6 * rows:] + mm(high, matrix_low, NT)
+    slot_lane = lax.broadcasted_iota(jnp.int32, (1, total_slots), 1)
+    back = jnp.zeros((rows, total_slots), jnp.float32)
+    for k in range(6):
+        first = k * slot_len if k < 5 else LANES
+        inside = (slot_lane >= first) & (slot_lane < first + slot_len)
+        back = jnp.where(inside, product[k * rows:(k + 1) * rows], back)
+    place = place[:, :total_slots]
     stiffness = mm(stacked(back), place, NT)
     stiffness = stiffness[:rows] + stiffness[rows:]
     result = stiff_coef * stiffness / area + long_range
@@ -231,9 +259,10 @@
         return carry
 
     lax.fori_loop(1, n, sent, 0)
+    for k in spans:
+        value_copy(k).wait_send()
     for k in range(5):
-        value_copy(k).wait_send()
-        term_copy(k).wait_send()
+        matrix_copy(k).wait_send()
 
 
 def per_device(position, order_field, cell_area, slot_vertex, send_count, corner_slot, edge_weight):
@@ -257,11 +286,11 @@
             *(pltpu.VMEM(x.shape, x.dtype) for x in args),
             pltpu.VMEM((n, rows, LANES), jnp.float32),
             pltpu.VMEM((rows, LANES), jnp.float32),
-            pltpu.VMEM((5, rows, LANES), jnp.float32),
-            pltpu.VMEM((rows, LANES), jnp.float32),
-            pltpu.VMEM((5, rows, LANES), jnp.float32),
+            pltpu.VMEM((wide, rows, LANES), jnp.float32),
+            pltpu.VMEM((LANES + PAD, LANES + PAD), jnp.float32),
+            pltpu.VMEM((LANES + PAD, LANES + PAD), jnp.float32),
             pltpu.VMEM((3, LANES, LANES), jnp.float32),
-            dma((7,)), dma((n,)), dma((n,)), dma((5,)), dma((5,)), dma((5,)), dma((5,)),
+            dma((7,)), dma((n,)), dma((n,)), dma((wide,)), dma((wide,)), dma((5,)), dma((5,)),
         ],
         compiler_params=pltpu.CompilerParams(collective_id=0, has_side_effects=True),
     )(*args)

time: 17.8 us -> 21.2 us (1.19)
  Pallas kernels: 17 us -> 20.4 us
    pallas_call x1, Pallas kernels: 17 us -> 20.4 us  [per_device(): pl.pallas_call(functools.partial(kernel, wide, blk, fields, slot_len), ou...]
where the time goes in v3:
time: 21.2 us; the launch traced here: 21 us
  Pallas kernels  20.4 us (96%)
  other arithmetic  0.6 us (3%)
    pallas_call x1, Pallas kernels, per_device(): pl.pallas_call(functools.partial(kernel, wide, blk, fields, slot_len), ou...  20.4 us
    add x1, other arithmetic, per_device(): return order_field ** 3 - order_field + extra  0.6 us

profile of v3, /device:TPU:0, one launch (start us, length us, event | category | flops | bytes accessed | tf_op | source)
XLA Modules:
  0.0 21.0 jit_solution(11386179074941173970)
XLA Ops:
  0.0 0.0 copy-start
  0.0 20.4 %shard_map.73 = f32[12,128]{1,0:T(8,128)S(1)} custom-call(f32[3,128]{1,0:T(4,128)} %pos_hbm.1, f32[12,128]{1,0:T(8,128)} %order_hbm.1, f32[1,128]{1,0:T(1,128)} %bitcast.5, s32[1,1,16,24]{3,2,1,0:T(8,128)} %slot_hbm.1, s32[1,1,16]{2,1,0:T(1,128)} %count_hbm.1, s32[3,1,256]{2,1,0:T(1,128)} %bitcast.3, f32[3,1,256]{2,1,0:T(1,128)} %bitcast.4), custom_call_target="tpu_custom_call" | custom-call | tf_op jit(solution)/shard_map/pallas_call | solution.py:280
  20.4 0.0 copy-done
  20.4 0.6 %fusion = f32[12,128]{1,0:T(8,128)} fusion(f32[12,128]{1,0:T(8,128)S(1)} %shard_map.73, f32[12,128]{1,0:T(8,128)S(1)} %copy-done), kind=kLoop, calls=%fused_computation.1 | loop fusion | flops 6144 | bytes 18432 | tf_op jit(solution)/shard_map/add | solution.py:297
Async XLA Ops:
  0.0 20.4 %copy-start = (f32[12,128]{1,0:T(8,128)S(1)}, f32[12,128]{1,0:T(8,128)}, u32[]{:S(2)}) copy-start(f32[12,128]{1,0:T(8,128)} %order_hbm.1) | copy-start | bytes 18436

commit v4 on v2

--- a/solution.py
+++ b/solution.py
@@ -9,6 +9,7 @@
 
 stiff_coef = 0.1
 LANES = 128
+PAD = 32
 GROUP = 4
 MESH = pl.DeviceIdType.MESH
 NT = (((1,), (1,)), ((), ()))
@@ -44,6 +45,7 @@
     soften = 4.0 / (n * LANES)
     strength = float(n * LANES) ** (-0.5)
     offsets = (1, wide - 1, 2, wide - 2, wide // 2)
+    total_slots = LANES + PAD
 
     def device(step):
         to = lax.rem(me + step, n)
@@ -100,13 +102,6 @@
     vout[...] = outgoing[:, :LANES]
     own_values = outgoing[:, LANES:]
 
-    columns = own.T
-    for k in range(3):
-        targets[k] = jnp.broadcast_to(columns[:, fields + k:fields + k + 1], (LANES, LANES))
-    row_id = lax.broadcasted_iota(jnp.int32, (rows, 1), 0)
-    center = jnp.sum(own * area, axis=1, keepdims=True) / jnp.sum(area)
-    center = jnp.where(row_id < fields, center, 0.0)
-
     def value_copy(k):
         return pltpu.make_async_remote_copy(
             src_ref=vout, dst_ref=vbuf.at[k], send_sem=vsend.at[k], recv_sem=vrecv.at[k],
@@ -124,6 +119,16 @@
             src_ref=blocks.at[0], dst_ref=blocks.at[step], send_sem=bsend.at[step],
             recv_sem=brecv.at[step], device_id=device(step), device_id_type=MESH,
         )
+
+    pl.semaphore_wait(barrier, n - 1)
+    for k in range(5):
+        value_copy(k).start()
+
+    def start_block(step, carry):
+        block_copy(step).start()
+        return carry
+
+    lax.fori_loop(1, n, start_block, 0)
 
     corner_rows = []
     for c in range(3):
@@ -134,20 +139,26 @@
             first = k * slot_len if offset else LANES
             column = jnp.where((corner >= low) & (corner < low + slot_len), corner - low + first, column)
         corner_rows.append(column)
-    elements = corner_rows[0].shape[1]
-    column = jnp.concatenate(corner_rows, axis=1)
-    column_id = lax.broadcasted_iota(jnp.int32, (2 * LANES, 3 * elements), 0)
-    pick = jnp.where(column_id == column, 1.0, 0.0).astype(jnp.bfloat16)
-
-    pl.semaphore_wait(barrier, n - 1)
-    for k in range(5):
-        value_copy(k).start()
-
-    def start_block(step, carry):
-        block_copy(step).start()
-        return carry
-
-    lax.fori_loop(1, n, start_block, 0)
+    column_id = lax.broadcasted_iota(jnp.int32, (total_slots, 1), 0)
+    picks = [jnp.where(column_id == column, 1.0, 0.0) for column in corner_rows]
+    signs, heavy, light = [], [], []
+    for c in range(3):
+        edge = picks[(c + 1) % 3] - picks[(c + 2) % 3]
+        hi, lo = (half.astype(jnp.float32) for half in halves(weight_ref[c]))
+        signs.append(edge.astype(jnp.bfloat16))
+        heavy.append((edge * hi).astype(jnp.bfloat16))
+        light.append((edge * lo).astype(jnp.bfloat16))
+    signs = jnp.concatenate(signs, axis=1)
+    matrix = mm(jnp.concatenate(heavy, axis=1), signs, NT)
+    matrix = matrix + mm(jnp.concatenate(light, axis=1), signs, NT)
+    matrix_high, matrix_low = halves(matrix)
+
+    columns = own.T
+    for k in range(3):
+        targets[k] = jnp.broadcast_to(columns[:, fields + k:fields + k + 1], (LANES, LANES))
+    row_id = lax.broadcasted_iota(jnp.int32, (rows, 1), 0)
+    center = jnp.sum(own * area, axis=1, keepdims=True) / jnp.sum(area)
+    center = jnp.where(row_id < fields, center, 0.0)
 
     part_lane = lax.broadcasted_iota(jnp.int32, (1, LANES), 1)
 
@@ -160,19 +171,10 @@
 
     for k in range(5):
         value_copy(k).wait_recv()
-    values = jnp.concatenate([merged(vbuf), own_values], axis=1)
-    picked = mm(stacked(values), pick, NN)
-    picked = picked[:rows] + picked[rows:]
-    value_a, value_b, value_c = (picked[:, c * elements:(c + 1) * elements] for c in range(3))
-    weight_a, weight_b, weight_c = (weight_ref[c] for c in range(3))
-    along_ab = weight_c * (value_a - value_b)
-    along_ac = weight_b * (value_a - value_c)
-    along_bc = weight_a * (value_b - value_c)
-    terms = jnp.concatenate(
-        [along_ab + along_ac, along_bc - along_ab, -along_ac - along_bc], axis=1
-    )
-    returned = mm(stacked(terms), pick, NT)
-    returned = returned[:rows] + returned[rows:]
+    values = jnp.concatenate([merged(vbuf), own_values[:, :PAD]], axis=1)
+    high, low = halves(values)
+    returned = mm(jnp.concatenate([high, low], axis=0), matrix_high, NN)
+    returned = returned[:rows] + returned[rows:] + mm(high, matrix_low, NN)
     rout[...] = returned[:, :LANES]
     own_terms = returned[:, LANES:]
 
@@ -218,19 +220,19 @@
     shift = sums / sums[fields + 3:]
     long_range = -strength * (total - shift * total[fields + 3:])
 
+    def sent(step, carry):
+        block_copy(step).wait_send()
+        return carry
+
+    lax.fori_loop(1, n, sent, 0)
     for k in range(5):
         term_copy(k).wait_recv()
     back = jnp.concatenate([merged(rbuf), own_terms], axis=1)
-    stiffness = mm(stacked(back), place, NT)
+    stiffness = mm(stacked(back), place[:, :total_slots], NT)
     stiffness = stiffness[:rows] + stiffness[rows:]
     result = stiff_coef * stiffness / area + long_range
     out_ref[...] = result[:fields]
 
-    def sent(step, carry):
-        block_copy(step).wait_send()
-        return carry
-
-    lax.fori_loop(1, n, sent, 0)
     for k in range(5):
         value_copy(k).wait_send()
         term_copy(k).wait_send()

time: 17.8 us -> 17.5 us (0.983)
  Pallas kernels: 17 us -> 16.8 us
    pallas_call x1, Pallas kernels: 17 us -> 16.8 us  [per_device(): pl.pallas_call(functools.partial(kernel, wide, blk, fields, slot_len), ou...]
where the time goes in v4:
time: 17.5 us; the launch traced here: 17.4 us
  Pallas kernels  16.8 us (96%)
  other arithmetic  0.6 us (3%)
    pallas_call x1, Pallas kernels, per_device(): pl.pallas_call(functools.partial(kernel, wide, blk, fields, slot_len), ou...  16.8 us
    add x1, other arithmetic, per_device(): return order_field ** 3 - order_field + extra  0.6 us

profile of v4, /device:TPU:0, one launch (start us, length us, event | category | flops | bytes accessed | tf_op | source)
XLA Modules:
  0.0 17.4 jit_solution(9016877140189336019)
XLA Ops:
  0.0 0.0 copy-start
  0.0 16.8 %shard_map.73 = f32[12,128]{1,0:T(8,128)S(1)} custom-call(f32[3,128]{1,0:T(4,128)} %pos_hbm.1, f32[12,128]{1,0:T(8,128)} %order_hbm.1, f32[1,128]{1,0:T(1,128)} %bitcast.5, s32[1,1,16,24]{3,2,1,0:T(8,128)} %slot_hbm.1, s32[1,1,16]{2,1,0:T(1,128)} %count_hbm.1, s32[3,1,256]{2,1,0:T(1,128)} %bitcast.3, f32[3,1,256]{2,1,0:T(1,128)} %bitcast.4), custom_call_target="tpu_custom_call" | custom-call | tf_op jit(solution)/shard_map/pallas_call | solution.py:253
  16.8 0.0 copy-done
  16.8 0.6 %fusion = f32[12,128]{1,0:T(8,128)} fusion(f32[12,128]{1,0:T(8,128)S(1)} %shard_map.73, f32[12,128]{1,0:T(8,128)S(1)} %copy-done), kind=kLoop, calls=%fused_computation.1 | loop fusion | flops 6144 | bytes 18432 | tf_op jit(solution)/shard_map/add | solution.py:270
Async XLA Ops:
  0.0 16.8 %copy-start = (f32[12,128]{1,0:T(8,128)S(1)}, f32[12,128]{1,0:T(8,128)}, u32[]{:S(2)}) copy-start(f32[12,128]{1,0:T(8,128)} %order_hbm.1) | copy-start | bytes 18436
